TPU v7x, 512 devices: a whole 4x8x8 slice. The times are simulated.
512 devices in a mesh: freq: 128 (over z, y, core), panel: 4 (over x).
Axes of the slice: x: 4, y: 8, z: 8, core: 2. Of those that a mesh axis runs over, the one named last changes fastest.
Arguments:
- wave: bfloat16 [2, 128, 1600, 1600], P(None, 'freq', 'panel'), may hold values from -0.15625 to 0.15625
- observed: float32 [4, 6400, 512], P('panel', 'freq'), may hold values from -25 to 25
Outputs:
- solution: float32 [25600, 512], P('freq')
All inputs are finite; a program needn't handle non-finite values.
Results may differ from a plain program's by a relative error of at most 0.0085.
Values may be sent and summed in bfloat16 or wider, within the bound.
A program may use at most 64 MiB of HBM per device.

v0:
```python
import math
import jax
import jax.numpy as jnp
from jax import lax
from jax.sharding import PartitionSpec as P

VS = 16
ITERS = 3
precise = lax.Precision.HIGHEST
epsilon = 1e-06


def transform_tables(freq_total, samples):
    freq_index = lax.broadcasted_iota(jnp.int32, (freq_total, samples), 0) + 1
    time_index = lax.broadcasted_iota(jnp.int32, (freq_total, samples), 1)
    phases = (freq_index * time_index % samples).astype(jnp.float32) * (2.0 * math.pi / samples)
    factor = math.sqrt(2.0 / samples)
    return jnp.stack([factor * jnp.cos(phases), -factor * jnp.sin(phases)])


def spectrum_flat(rows, table):
    return jnp.einsum("cft,rt->fcr", table, rows, precision=precise).reshape(-1)


def owner_layout(received, blocks, local_freqs):
    pieces = received.reshape(blocks, local_freqs, 2, -1).transpose(2, 1, 0, 3)
    return pieces.reshape(2, local_freqs, -1)


def trace_layout(spectrum, blocks):
    parts, local_freqs, total_rows = spectrum.shape
    pieces = spectrum.reshape(parts, local_freqs, blocks, total_rows // blocks).transpose(
        2, 1, 0, 3
    )
    return pieces.reshape(-1)


def time_traces(received, table, blocks, local_freqs):
    pieces = received.reshape(blocks, local_freqs, 2, -1).astype(jnp.float32)
    folded = table.reshape(2, blocks, local_freqs, table.shape[2])
    return jnp.einsum("jlcr,cjlt->rt", pieces, folded, precision=precise)


def forward_product(spectrum, wave):

    def product_of(left, right):
        return jnp.einsum("fvs,frs->fvr", left, right, preferred_element_type=jnp.float32)

    real_out = product_of(spectrum[0], wave[0]) - product_of(spectrum[1], wave[1])
    imag_out = product_of(spectrum[0], wave[1]) + product_of(spectrum[1], wave[0])
    return jnp.stack([real_out, imag_out]).astype(jnp.bfloat16)


def adjoint_product(spectrum, wave):

    def product_of(left, right):
        return jnp.einsum("fvr,frs->fvs", left, right, preferred_element_type=jnp.float32)

    real_out = product_of(spectrum[0], wave[0]) + product_of(spectrum[1], wave[1])
    imag_out = product_of(spectrum[1], wave[0]) - product_of(spectrum[0], wave[1])
    return jnp.stack([real_out, imag_out])


def on_device(wave, observed):
    local_freqs = wave.shape[1]
    panel_rows = wave.shape[2]
    blocks = lax.axis_size("freq")
    freq_total = local_freqs * blocks
    samples = observed.shape[2]
    table = transform_tables(freq_total, samples)

    def summed_panels(partial_sum):
        return lax.psum(partial_sum, "panel")

    def adjoint(data):
        lines = spectrum_flat(data, table).astype(jnp.bfloat16)
        moved_in = lax.all_to_all(lines, "freq", split_axis=0, concat_axis=0, tiled=True)
        spectrum = owner_layout(moved_in, blocks, local_freqs).reshape(
            2, local_freqs, VS, panel_rows
        )
        partial_sum = adjoint_product(spectrum, wave)
        total = summed_panels(partial_sum).reshape(2, local_freqs, -1)
        moved = lax.all_to_all(
            trace_layout(total, blocks), "freq", split_axis=0, concat_axis=0, tiled=True
        )
        return time_traces(moved, table, blocks, local_freqs)

    def data_norm(field):
        return jnp.sqrt(lax.psum(jnp.sum(field * field), ("freq", "panel")) + epsilon)

    def model_norm(field):
        return jnp.sqrt(lax.psum(jnp.sum(field * field), "freq") + epsilon)

    data_vector = observed[0]
    beta = data_norm(data_vector)
    data_vector = data_vector / beta
    model_vector = adjoint(data_vector)
    alpha = model_norm(model_vector)
    model_vector = model_vector / alpha
    direction = model_vector
    solution = jnp.zeros_like(model_vector)
    phi_bar = beta
    rho_bar = alpha
    for step in range(ITERS):
        forward_lines = spectrum_flat(model_vector, table).astype(jnp.bfloat16)
        forward_moved_in = lax.all_to_all(
            forward_lines, "freq", split_axis=0, concat_axis=0, tiled=True
        )
        forward_spectrum = owner_layout(forward_moved_in, blocks, local_freqs).reshape(
            2, local_freqs, VS, -1
        )
        product = forward_product(forward_spectrum, wave).reshape(2, local_freqs, -1)
        forward_moved = lax.all_to_all(
            trace_layout(product, blocks), "freq", split_axis=0, concat_axis=0, tiled=True
        )
        data_vector = time_traces(forward_moved, table, blocks, local_freqs) - alpha * data_vector
        beta = data_norm(data_vector)
        data_vector = data_vector / beta
        model_vector = adjoint(data_vector) - beta * model_vector
        alpha = model_norm(model_vector)
        model_vector = model_vector / alpha
        rho_new = jnp.sqrt(rho_bar * rho_bar + beta * beta)
        cosine = rho_bar / rho_new
        sine_part = beta / rho_new
        theta = sine_part * alpha
        rho_bar = -cosine * alpha
        phi_value = cosine * phi_bar
        phi_bar = sine_part * phi_bar
        solution = solution + phi_value / rho_new * direction
        direction = model_vector - theta / rho_new * direction
    return solution


def solution(mesh):
    placed = (P(None, "freq", "panel", None), P("panel", "freq", None))
    return jax.shard_map(
        on_device, mesh=mesh, in_specs=placed, out_specs=P("freq", None), check_vma=False
    )
```

profile of v0, /device:TPU:1, one launch (start us, length us, event | category | flops | bytes accessed | tf_op | source)
XLA Modules:
  0.0 1600.5 jit_solution(7903671710847964002)
XLA Ops:
  6.5 1.9 multiply_reduce_fusion.5
  8.4 106.0 %psum.70 = f32[]{:T(128)} all-reduce(f32[]{:T(128)} %multiply_reduce_fusion.5), channel_id=1, replica_groups=mesh['freq'=128,'panel'=4] {'freq','panel'}, use_global_device_ids=true, to_apply=%region_1.2 | all-reduce | flops 1 | bytes 8 | tf_op jit(solution)/shard_map/psum | solution.py:89
  115.1 1.1 cosine_multiply_fusion
  117.0 1.5 fusion.72
  118.6 20.5 %all_to_all.90 = bf16[128,100,1]{1,2,0:T(2,128)(2,1)S(1)} all-to-all(bf16[128,100,1]{1,2,0:T(2,128)(2,1)S(1)} %copy.37), channel_id=1, replica_groups=mesh['freq'=128,'panel'=4] {'freq'}, dimensions={0} | all-to-all | bytes 51200 | tf_op jit(solution)/shard_map/all_to_all | solution.py:77
  139.7 1.6 fusion.44
  143.3 40.2 %all-reduce.4.cloned.1.call-done = f32[128,400,1]{0,1,2:T(8,128)} async-done(((f32[128,400,1]{0,1,2:T(8,128)}), f32[128,400,1]{0,1,2:T(8,128)}) %all-reduce.4.cloned.1.call-update) | async-done | bytes 204816 | tf_op jit(solution)/shard_map/psum | solution.py:73
  183.5 1.1 copy.42
  184.6 31.3 %all_to_all.91 = f32[128,400,1]{1,2,0:T(1,128)S(1)} all-to-all(f32[128,400,1]{1,2,0:T(1,128)S(1)} %copy.42), channel_id=1, replica_groups=mesh['freq'=128,'panel'=4] {'freq'}, dimensions={0} | all-to-all | bytes 409600 | tf_op jit(solution)/shard_map/all_to_all | solution.py:83
  216.0 2.2 multiply_reduce_fusion.2
  218.3 247.2 %psum.72 = f32[]{:T(128)} all-reduce(f32[]{:T(128)} %get-tuple-element.19), channel_id=1, replica_groups=mesh['freq'=128,'panel'=4] {'freq'}, use_global_device_ids=true, to_apply=%region_4.5 | all-reduce | flops 1 | bytes 8 | tf_op jit(solution)/shard_map/psum | solution.py:92
  466.1 1.7 convolution_convert_fusion.2
  468.6 1.5 reduce.1
  470.3 19.2 %all_to_all.92 = bf16[128,2,200]{2,1,0:T(2,128)(2,1)S(1)} all-to-all(bf16[128,2,200]{2,1,0:T(2,128)(2,1)S(1)} %reshape.643), channel_id=1, replica_groups=mesh['freq'=128,'panel'=4] {'freq'}, dimensions={0} | all-to-all | bytes 204800 | tf_op jit(solution)/shard_map/all_to_all | solution.py:106
  494.5 16.5 %all_to_all.93 = bf16[128,100,1]{1,2,0:T(2,128)(2,1)S(1)} all-to-all(bf16[128,100,1]{1,2,0:T(2,128)(2,1)S(1)} %reshape.640), channel_id=1, replica_groups=mesh['freq'=128,'panel'=4] {'freq'}, dimensions={0} | all-to-all | bytes 51200 | tf_op jit(solution)/shard_map/all_to_all | solution.py:113
  511.2 1.9 multiply_reduce_fusion.4
  513.1 94.5 %psum.73 = f32[]{:T(128)} all-reduce(f32[]{:T(128)} %get-tuple-element.21), channel_id=1, replica_groups=mesh['freq'=128,'panel'=4] {'freq','panel'}, use_global_device_ids=true, to_apply=%region_6.7 | all-reduce | flops 1 | bytes 8 | tf_op jit(solution)/shard_map/psum | solution.py:89
  608.4 1.5 fusion.73
  610.1 19.3 %all_to_all.94 = bf16[128,100,1]{1,2,0:T(2,128)(2,1)S(1)} all-to-all(bf16[128,100,1]{1,2,0:T(2,128)(2,1)S(1)} %copy.53), channel_id=1, replica_groups=mesh['freq'=128,'panel'=4] {'freq'}, dimensions={0} | all-to-all | bytes 51200 | tf_op jit(solution)/shard_map/all_to_all | solution.py:77
  632.3 40.8 %all-reduce.6.cloned.1.call-done = f32[128,400,1]{0,1,2:T(8,128)} async-done(((f32[128,400,1]{0,1,2:T(8,128)}), f32[128,400,1]{0,1,2:T(8,128)}) %all-reduce.6.cloned.1.call-update) | async-done | bytes 204816 | tf_op jit(solution)/shard_map/psum | solution.py:73
  673.1 1.1 copy.58
  674.2 31.4 %all_to_all.95 = f32[128,400,1]{1,2,0:T(1,128)} all-to-all(f32[128,400,1]{1,2,0:T(1,128)S(1)} %copy.58), channel_id=1, replica_groups=mesh['freq'=128,'panel'=4] {'freq'}, dimensions={0} | all-to-all | bytes 409600 | tf_op jit(solution)/shard_map/all_to_all | solution.py:83
  705.6 1.1 copy.59
  706.7 2.9 multiply_reduce_fusion.1
  709.7 247.2 %psum.75 = f32[]{:T(128)} all-reduce(f32[]{:T(128)} %get-tuple-element.23), channel_id=1, replica_groups=mesh['freq'=128,'panel'=4] {'freq'}, use_global_device_ids=true, to_apply=%region_9.10 | all-reduce | flops 1 | bytes 8 | tf_op jit(solution)/shard_map/psum | solution.py:92
  957.6 1.8 convolution_convert_fusion.1
  959.6 1.5 reduce.2
  961.2 19.2 %all_to_all.96 = bf16[128,2,200]{2,1,0:T(2,128)(2,1)S(1)} all-to-all(bf16[128,2,200]{2,1,0:T(2,128)(2,1)S(1)} %reshape.645), channel_id=1, replica_groups=mesh['freq'=128,'panel'=4] {'freq'}, dimensions={0} | all-to-all | bytes 204800 | tf_op jit(solution)/shard_map/all_to_all | solution.py:106
  982.1 1.0 copy.62
  985.5 16.5 %all_to_all.97 = bf16[128,100,1]{1,2,0:T(2,128)(2,1)S(1)} all-to-all(bf16[128,100,1]{1,2,0:T(2,128)(2,1)S(1)} %reshape.641), channel_id=1, replica_groups=mesh['freq'=128,'panel'=4] {'freq'}, dimensions={0} | all-to-all | bytes 51200 | tf_op jit(solution)/shard_map/all_to_all | solution.py:113
  1002.1 1.9 multiply_reduce_fusion.3
  1004.1 94.5 %psum.76 = f32[]{:T(128)} all-reduce(f32[]{:T(128)} %get-tuple-element.25), channel_id=1, replica_groups=mesh['freq'=128,'panel'=4] {'freq','panel'}, use_global_device_ids=true, to_apply=%region_11.12 | all-reduce | flops 1 | bytes 8 | tf_op jit(solution)/shard_map/psum | solution.py:89
  1099.3 1.5 fusion.74
  1101.0 19.3 %all_to_all.98 = bf16[128,100,1]{1,2,0:T(2,128)(2,1)S(1)} all-to-all(bf16[128,100,1]{1,2,0:T(2,128)(2,1)S(1)} %copy.69), channel_id=1, replica_groups=mesh['freq'=128,'panel'=4] {'freq'}, dimensions={0} | all-to-all | bytes 51200 | tf_op jit(solution)/shard_map/all_to_all | solution.py:77
  1123.1 40.9 %all-reduce.8.cloned.1.call-done = f32[128,400,1]{0,1,2:T(8,128)} async-done(((f32[128,400,1]{0,1,2:T(8,128)}), f32[128,400,1]{0,1,2:T(8,128)}) %all-reduce.8.cloned.1.call-update) | async-done | bytes 204816 | tf_op jit(solution)/shard_map/psum | solution.py:73
  1164.1 1.1 copy.74
  1165.1 31.6 %all_to_all.99 = f32[128,400,1]{1,2,0:T(1,128)} all-to-all(f32[128,400,1]{1,2,0:T(1,128)S(1)} %copy.74), channel_id=1, replica_groups=mesh['freq'=128,'panel'=4] {'freq'}, dimensions={0} | all-to-all | bytes 409600 | tf_op jit(solution)/shard_map/all_to_all | solution.py:83
  1196.8 1.1 copy.75
  1197.9 3.1 multiply_reduce_fusion
  1201.0 247.0 %psum.78 = f32[]{:T(128)} all-reduce(f32[]{:T(128)} %get-tuple-element.27), channel_id=1, replica_groups=mesh['freq'=128,'panel'=4] {'freq'}, use_global_device_ids=true, to_apply=%region_14.15 | all-reduce | flops 1 | bytes 8 | tf_op jit(solution)/shard_map/psum | solution.py:92
  1448.7 1.8 convolution_convert_fusion
  1450.7 1.5 reduce.3
  1452.3 19.2 %all_to_all.100 = bf16[128,2,200]{2,1,0:T(2,128)(2,1)S(1)} all-to-all(bf16[128,2,200]{2,1,0:T(2,128)(2,1)S(1)} %reshape.647), channel_id=1, replica_groups=mesh['freq'=128,'panel'=4] {'freq'}, dimensions={0} | all-to-all | bytes 204800 | tf_op jit(solution)/shard_map/all_to_all | solution.py:106
  1477.2 5.5 all-to-all-start.11
  1483.1 11.1 all-to-all-done.11
  1494.4 2.0 fusion.93
  1496.4 94.5 %psum.79 = f32[]{:T(128)} all-reduce(f32[]{:T(128)} %fusion.93), channel_id=1, replica_groups=mesh['freq'=128,'panel'=4] {'freq','panel'}, use_global_device_ids=true, to_apply=%region_16.17 | all-reduce | flops 1 | bytes 8 | tf_op jit(solution)/shard_map/psum | solution.py:89
  1591.7 2.1 multiply_add_fusion
  (141 shorter events, 25.9 us)
Async XLA Ops:
  6.5 134.8 %copy-start = (bf16[2,1,400,1600]{3,2,1,0:T(8,128)(2,1)S(1)}, bf16[2,1,400,1600]{3,2,1,0:T(8,128)(2,1)}, u32[]{:S(2)}) copy-start(bf16[2,1,400,1600]{3,2,1,0:T(8,128)(2,1)} %param.2) | copy-start | bytes 7680004
  6.5 177.0 %all-reduce.4.cloned.1.call-start = ((), (), s32[]{:S(2)}) async-start(), calls=%async_computation.12 | async-start | bytes 409600 | tf_op jit(solution)/shard_map/psum | solution.py:73
  116.3 0.7 copy-start.7
  116.3 25.6 %copy-start.1 = (f32[1,128,512]{2,1,0:T(8,128)}, f32[1,128,512]{2,1,0:T(8,128)S(1)}, u32[]{:S(2)}) copy-start(f32[1,128,512]{2,1,0:T(8,128)S(1)} %get-tuple-element.17) | copy-start | bytes 786436
  143.3 529.8 %all-reduce.6.cloned.1.call-start = ((), (), s32[]{:S(2)}) async-start(), calls=%async_computation.13 | async-start | bytes 409600 | tf_op jit(solution)/shard_map/psum | solution.py:73
  491.2 20.0 %copy-start.2 = (f32[1,128,512]{2,1,0:T(8,128)S(1)}, f32[1,128,512]{2,1,0:T(8,128)}, u32[]{:S(2)}) copy-start(f32[1,128,512]{2,1,0:T(8,128)} %copy-done.1) | copy-start | bytes 786436
  513.1 117.7 %copy-start.9 = (f32[50,512]{1,0:T(8,128)}, f32[50,512]{1,0:T(8,128)S(1)}, u32[]{:S(2)}) copy-start(f32[50,512]{1,0:T(8,128)S(1)} %get-tuple-element.22) | copy-start | bytes 307204
  632.2 531.8 %all-reduce.8.cloned.1.call-start = ((), (), s32[]{:S(2)}) async-start(), calls=%async_computation.14 | async-start | bytes 409600 | tf_op jit(solution)/shard_map/psum | solution.py:73
  705.6 252.0 %copy-start.3 = (f32[1,128,512]{2,1,0:T(8,128)S(1)}, f32[1,128,512]{2,1,0:T(8,128)}, u32[]{:S(2)}) copy-start(f32[1,128,512]{2,1,0:T(8,128)} %copy-done.1) | copy-start | bytes 786436
  982.1 20.0 %copy-start.4 = (f32[1,128,512]{2,1,0:T(8,128)S(1)}, f32[1,128,512]{2,1,0:T(8,128)}, u32[]{:S(2)}) copy-start(f32[1,128,512]{2,1,0:T(8,128)} %copy-done.1) | copy-start | bytes 786436
  1004.1 117.7 %copy-start.8 = (f32[50,512]{1,0:T(8,128)}, f32[50,512]{1,0:T(8,128)S(1)}, u32[]{:S(2)}) copy-start(f32[50,512]{1,0:T(8,128)S(1)} %get-tuple-element.26) | copy-start | bytes 307204
  1196.8 251.9 %copy-start.5 = (f32[1,128,512]{2,1,0:T(8,128)S(1)}, f32[1,128,512]{2,1,0:T(8,128)}, u32[]{:S(2)}) copy-start(f32[1,128,512]{2,1,0:T(8,128)} %copy-done.1) | copy-start | bytes 786436
  1473.2 21.2 %copy-start.6 = (f32[1,128,512]{2,1,0:T(8,128)S(1)}, f32[1,128,512]{2,1,0:T(8,128)}, u32[]{:S(2)}) copy-start(f32[1,128,512]{2,1,0:T(8,128)} %copy-done.1) | copy-start | bytes 786436
  1477.2 17.1 %all-to-all-start.11 = ((bf16[128,100,1]{1,2,0:T(2,128)(2,1)}), bf16[128,100,1]{1,2,0:T(2,128)(2,1)S(1)}, u32[]{:S(2)}, u32[]{:S(2)}) async-start(bf16[128,100,1]{1,2,0:T(2,128)(2,1)} %reshape.642), calls=%async_computation.11 | async-start | bytes 131072 | tf_op jit(solution)/shard_map/all_to_all | solution.py:113
Sparse Core Ops, SparseCore 0:
  143.4 40.0 all-reduce.3
  632.4 40.7 all-reduce.5
  1123.3 40.7 all-reduce.7
where the time goes:
time: 1610 us; the launch traced here: 1600 us
  blocking collectives  1380 us (86%)
  waiting for transfers between devices  133 us (8%)
  matrix products  34.4 us (2%)
  local copies, waits for them, and re-layouts  23 us (1%)
  between operations  19.3 us (1%)
    psum x3, blocking collectives, model_norm(): return jnp.sqrt(lax.psum(jnp.sum(field * field), 'freq') + epsilon)  741 us
    psum x4, blocking collectives, data_norm(): lax.psum(jnp.sum(field * field), ('freq', 'panel')) + epsilon  390 us
    psum x3, waiting for transfers between devices, summed_panels(): return lax.psum(partial_sum, 'panel')  122 us
    all_to_all x3, blocking collectives, adjoint(): lax.all_to_all(trace_layout(total, blocks), 'freq', split_axis=0, concat_...  94.4 us
    all_to_all x3, blocking collectives, adjoint(): lax.all_to_all(lines, 'freq', split_axis=0, concat_axis=0, tiled=True)  59.1 us
    all_to_all x3, blocking collectives, on_device(): lax.all_to_all(forward_lines, 'freq', split_axis=0, concat_axis=0, tiled=...  57.7 us
    all_to_all x2, blocking collectives, on_device(): lax.all_to_all(trace_layout(product, blocks), 'freq', split_axis=0, conca...  33 us
  transfers between devices with their start and end apart: 4, of which 4 were waited for; matrix products, arithmetic and copies ran while one was open for 0% of the time, Pallas kernels for 0%

commit v1 on v0

--- a/solution.py
+++ b/solution.py
@@ -1,3 +1,4 @@
+import functools
 import math
 import jax
 import jax.numpy as jnp
@@ -8,6 +9,13 @@
 ITERS = 3
 precise = lax.Precision.HIGHEST
 epsilon = 1e-06
+
+
+def mark_hubs(xs, axis_key):
+    return lax.all_gather(xs, axis_key).sum(axis=0)
+
+
+clear_bench = functools.partial(mark_hubs, axis_key="panel")
 
 
 def transform_tables(freq_total, samples):
@@ -70,7 +78,7 @@
     table = transform_tables(freq_total, samples)
 
     def summed_panels(partial_sum):
-        return lax.psum(partial_sum, "panel")
+        return clear_bench(partial_sum)
 
     def adjoint(data):
         lines = spectrum_flat(data, table).astype(jnp.bfloat16)

time: 1610 us -> 1480 us (0.919)
  waiting for transfers between devices: 133 us -> 11.1 us
    psum x3 -> x0, waiting for transfers between devices: 122 us -> none  [summed_panels(): return lax.psum(partial_sum, 'panel')]
    all_gather x0 -> x3, blocking collectives: none -> 33.5 us  [mark_hubs(): return lax.all_gather(xs, axis_key).sum(axis=0)]
    all_to_all x3, blocking collectives: 94.4 us -> 72 us  [adjoint(): lax.all_to_all(trace_layout(total, blocks), 'freq', split_axis=0, concat_...]
  transfers between devices with their start and end apart: 4 -> 1, of which waited for: 4 -> 1; matrix products, arithmetic and copies ran while one was open for 0% -> 0% of each run, Pallas kernels for 0% -> 0%
where the time goes in v1:
time: 1480 us; the launch traced here: 1470 us
  blocking collectives  1390 us (94%)
  matrix products  34.4 us (2%)
  local copies, waits for them, and re-layouts  18.2 us (1%)
    psum x3, blocking collectives, model_norm(): return jnp.sqrt(lax.psum(jnp.sum(field * field), 'freq') + epsilon)  741 us
    psum x4, blocking collectives, data_norm(): lax.psum(jnp.sum(field * field), ('freq', 'panel')) + epsilon  390 us
    all_to_all x3, blocking collectives, adjoint(): lax.all_to_all(trace_layout(total, blocks), 'freq', split_axis=0, concat_...  72 us
    all_to_all x3, blocking collectives, adjoint(): lax.all_to_all(lines, 'freq', split_axis=0, concat_axis=0, tiled=True)  59.1 us
    all_to_all x3, blocking collectives, on_device(): lax.all_to_all(forward_lines, 'freq', split_axis=0, concat_axis=0, tiled=...  57.7 us
    all_gather x3, blocking collectives, mark_hubs(): return lax.all_gather(xs, axis_key).sum(axis=0)  33.5 us
    all_to_all x2, blocking collectives, on_device(): lax.all_to_all(trace_layout(product, blocks), 'freq', split_axis=0, conca...  33 us
  transfers between devices with their start and end apart: 1, of which 1 were waited for; matrix products, arithmetic and copies ran while one was open for 0% of the time, Pallas kernels for 0%

profile of v1, /device:TPU:1, one launch (start us, length us, event | category | flops | bytes accessed | tf_op | source)
XLA Modules:
  0.0 1471.8 jit_solution(6590953463883659366)
XLA Ops:
  0.0 1.9 multiply_reduce_fusion.5
  1.9 106.0 %psum.49 = f32[]{:T(128)} all-reduce(f32[]{:T(128)} %multiply_reduce_fusion.5), channel_id=1, replica_groups=mesh['freq'=128,'panel'=4] {'freq','panel'}, use_global_device_ids=true, to_apply=%region_1.2 | all-reduce | flops 1 | bytes 8 | tf_op jit(solution)/shard_map/psum | solution.py:97
  108.6 1.1 cosine_multiply_fusion
  110.4 1.5 fusion.72
  112.1 20.5 %all_to_all.90 = bf16[128,100,1]{1,2,0:T(2,128)(2,1)S(1)} all-to-all(bf16[128,100,1]{1,2,0:T(2,128)(2,1)S(1)} %copy.34), channel_id=1, replica_groups=mesh['freq'=128,'panel'=4] {'freq'}, dimensions={0} | all-to-all | bytes 51200 | tf_op jit(solution)/shard_map/all_to_all | solution.py:85
  133.2 1.6 fusion.44
  135.7 11.0 all-gather
  147.2 23.8 %all_to_all.91 = f32[128,400,1]{1,2,0:T(1,128)S(1)} all-to-all(f32[128,400,1]{1,2,0:T(1,128)S(1)} %copy.39), channel_id=1, replica_groups=mesh['freq'=128,'panel'=4] {'freq'}, dimensions={0} | all-to-all | bytes 409600 | tf_op jit(solution)/shard_map/all_to_all | solution.py:91
  171.2 2.2 multiply_reduce_fusion.2
  173.4 247.2 %psum.50 = f32[]{:T(128)} all-reduce(f32[]{:T(128)} %get-tuple-element.19), channel_id=1, replica_groups=mesh['freq'=128,'panel'=4] {'freq'}, use_global_device_ids=true, to_apply=%region_4.5 | all-reduce | flops 1 | bytes 8 | tf_op jit(solution)/shard_map/psum | solution.py:100
  421.2 1.7 convolution_convert_fusion.2
  423.7 1.5 reduce.10
  425.4 19.2 %all_to_all.92 = bf16[128,2,200]{2,1,0:T(2,128)(2,1)S(1)} all-to-all(bf16[128,2,200]{2,1,0:T(2,128)(2,1)S(1)} %reshape.655), channel_id=1, replica_groups=mesh['freq'=128,'panel'=4] {'freq'}, dimensions={0} | all-to-all | bytes 204800 | tf_op jit(solution)/shard_map/all_to_all | solution.py:114
  446.3 1.0 copy.43
  449.6 16.5 %all_to_all.93 = bf16[128,100,1]{1,2,0:T(2,128)(2,1)S(1)} all-to-all(bf16[128,100,1]{1,2,0:T(2,128)(2,1)S(1)} %reshape.652), channel_id=1, replica_groups=mesh['freq'=128,'panel'=4] {'freq'}, dimensions={0} | all-to-all | bytes 51200 | tf_op jit(solution)/shard_map/all_to_all | solution.py:121
  466.3 1.9 multiply_reduce_fusion.4
  468.2 94.0 %psum.51 = f32[]{:T(128)} all-reduce(f32[]{:T(128)} %get-tuple-element.21), channel_id=1, replica_groups=mesh['freq'=128,'panel'=4] {'freq','panel'}, use_global_device_ids=true, to_apply=%region_6.7 | all-reduce | flops 1 | bytes 8 | tf_op jit(solution)/shard_map/psum | solution.py:97
  562.9 1.5 fusion.73
  564.6 19.3 %all_to_all.94 = bf16[128,100,1]{1,2,0:T(2,128)(2,1)S(1)} all-to-all(bf16[128,100,1]{1,2,0:T(2,128)(2,1)S(1)} %copy.50), channel_id=1, replica_groups=mesh['freq'=128,'panel'=4] {'freq'}, dimensions={0} | all-to-all | bytes 51200 | tf_op jit(solution)/shard_map/all_to_all | solution.py:85
  585.8 11.6 all-gather.1
  597.9 23.3 %all_to_all.95 = f32[128,400,1]{1,2,0:T(1,128)} all-to-all(f32[128,400,1]{1,2,0:T(1,128)S(1)} %copy.55), channel_id=1, replica_groups=mesh['freq'=128,'panel'=4] {'freq'}, dimensions={0} | all-to-all | bytes 409600 | tf_op jit(solution)/shard_map/all_to_all | solution.py:91
  621.1 1.1 copy.56
  622.3 3.0 multiply_reduce_fusion.1
  625.2 247.2 %psum.52 = f32[]{:T(128)} all-reduce(f32[]{:T(128)} %get-tuple-element.23), channel_id=1, replica_groups=mesh['freq'=128,'panel'=4] {'freq'}, use_global_device_ids=true, to_apply=%region_9.10 | all-reduce | flops 1 | bytes 8 | tf_op jit(solution)/shard_map/psum | solution.py:100
  873.2 1.8 convolution_convert_fusion.1
  875.1 1.5 reduce.11
  876.8 19.2 %all_to_all.96 = bf16[128,2,200]{2,1,0:T(2,128)(2,1)S(1)} all-to-all(bf16[128,2,200]{2,1,0:T(2,128)(2,1)S(1)} %reshape.657), channel_id=1, replica_groups=mesh['freq'=128,'panel'=4] {'freq'}, dimensions={0} | all-to-all | bytes 204800 | tf_op jit(solution)/shard_map/all_to_all | solution.py:114
  897.7 1.0 copy.59
  901.0 16.5 %all_to_all.97 = bf16[128,100,1]{1,2,0:T(2,128)(2,1)S(1)} all-to-all(bf16[128,100,1]{1,2,0:T(2,128)(2,1)S(1)} %reshape.653), channel_id=1, replica_groups=mesh['freq'=128,'panel'=4] {'freq'}, dimensions={0} | all-to-all | bytes 51200 | tf_op jit(solution)/shard_map/all_to_all | solution.py:121
  917.7 2.0 multiply_reduce_fusion.3
  919.6 95.4 %psum.53 = f32[]{:T(128)} all-reduce(f32[]{:T(128)} %get-tuple-element.25), channel_id=1, replica_groups=mesh['freq'=128,'panel'=4] {'freq','panel'}, use_global_device_ids=true, to_apply=%region_11.12 | all-reduce | flops 1 | bytes 8 | tf_op jit(solution)/shard_map/psum | solution.py:97
  1015.7 1.5 fusion.74
  1017.5 19.3 %all_to_all.98 = bf16[128,100,1]{1,2,0:T(2,128)(2,1)S(1)} all-to-all(bf16[128,100,1]{1,2,0:T(2,128)(2,1)S(1)} %copy.66), channel_id=1, replica_groups=mesh['freq'=128,'panel'=4] {'freq'}, dimensions={0} | all-to-all | bytes 51200 | tf_op jit(solution)/shard_map/all_to_all | solution.py:85
  1038.6 11.0 all-gather.2
  1050.1 24.9 %all_to_all.99 = f32[128,400,1]{1,2,0:T(1,128)} all-to-all(f32[128,400,1]{1,2,0:T(1,128)S(1)} %copy.71), channel_id=1, replica_groups=mesh['freq'=128,'panel'=4] {'freq'}, dimensions={0} | all-to-all | bytes 409600 | tf_op jit(solution)/shard_map/all_to_all | solution.py:91
  1075.1 1.1 copy.72
  1076.2 3.0 multiply_reduce_fusion
  1079.2 247.0 %psum.54 = f32[]{:T(128)} all-reduce(f32[]{:T(128)} %get-tuple-element.27), channel_id=1, replica_groups=mesh['freq'=128,'panel'=4] {'freq'}, use_global_device_ids=true, to_apply=%region_14.15 | all-reduce | flops 1 | bytes 8 | tf_op jit(solution)/shard_map/psum | solution.py:100
  1327.0 1.8 convolution_convert_fusion
  1328.9 1.5 reduce.12
  1330.6 19.2 %all_to_all.100 = bf16[128,2,200]{2,1,0:T(2,128)(2,1)S(1)} all-to-all(bf16[128,2,200]{2,1,0:T(2,128)(2,1)S(1)} %reshape.659), channel_id=1, replica_groups=mesh['freq'=128,'panel'=4] {'freq'}, dimensions={0} | all-to-all | bytes 204800 | tf_op jit(solution)/shard_map/all_to_all | solution.py:114
  1351.5 1.0 copy.75
  1354.7 0.7 reshape.654
  1355.4 5.6 all-to-all-start.11
  1361.4 11.1 all-to-all-done.11
  1372.7 2.0 fusion.93
  1374.7 94.0 %psum.55 = f32[]{:T(128)} all-reduce(f32[]{:T(128)} %fusion.93), channel_id=1, replica_groups=mesh['freq'=128,'panel'=4] {'freq','panel'}, use_global_device_ids=true, to_apply=%region_16.17 | all-reduce | flops 1 | bytes 8 | tf_op jit(solution)/shard_map/psum | solution.py:97
  1469.5 2.1 multiply_add_fusion
  (138 shorter events, 21.6 us)
Async XLA Ops:
  0.0 134.8 %copy-start = (bf16[2,1,400,1600]{3,2,1,0:T(8,128)(2,1)S(1)}, bf16[2,1,400,1600]{3,2,1,0:T(8,128)(2,1)}, u32[]{:S(2)}) copy-start(bf16[2,1,400,1600]{3,2,1,0:T(8,128)(2,1)} %param.2) | copy-start | bytes 7680004
  109.7 0.7 copy-start.7
  109.7 25.7 %copy-start.1 = (f32[1,128,512]{2,1,0:T(8,128)}, f32[1,128,512]{2,1,0:T(8,128)S(1)}, u32[]{:S(2)}) copy-start(f32[1,128,512]{2,1,0:T(8,128)S(1)} %get-tuple-element.17) | copy-start | bytes 786436
  446.3 20.0 %copy-start.2 = (f32[1,128,512]{2,1,0:T(8,128)S(1)}, f32[1,128,512]{2,1,0:T(8,128)}, u32[]{:S(2)}) copy-start(f32[1,128,512]{2,1,0:T(8,128)} %copy-done.1) | copy-start | bytes 786436
  468.2 117.2 %copy-start.9 = (f32[50,512]{1,0:T(8,128)}, f32[50,512]{1,0:T(8,128)S(1)}, u32[]{:S(2)}) copy-start(f32[50,512]{1,0:T(8,128)S(1)} %get-tuple-element.22) | copy-start | bytes 307204
  621.1 252.0 %copy-start.3 = (f32[1,128,512]{2,1,0:T(8,128)S(1)}, f32[1,128,512]{2,1,0:T(8,128)}, u32[]{:S(2)}) copy-start(f32[1,128,512]{2,1,0:T(8,128)} %copy-done.1) | copy-start | bytes 786436
  897.7 20.0 %copy-start.4 = (f32[1,128,512]{2,1,0:T(8,128)S(1)}, f32[1,128,512]{2,1,0:T(8,128)}, u32[]{:S(2)}) copy-start(f32[1,128,512]{2,1,0:T(8,128)} %copy-done.1) | copy-start | bytes 786436
  919.6 118.7 %copy-start.8 = (f32[50,512]{1,0:T(8,128)}, f32[50,512]{1,0:T(8,128)S(1)}, u32[]{:S(2)}) copy-start(f32[50,512]{1,0:T(8,128)S(1)} %get-tuple-element.26) | copy-start | bytes 307204
  1075.1 251.9 %copy-start.5 = (f32[1,128,512]{2,1,0:T(8,128)S(1)}, f32[1,128,512]{2,1,0:T(8,128)}, u32[]{:S(2)}) copy-start(f32[1,128,512]{2,1,0:T(8,128)} %copy-done.1) | copy-start | bytes 786436
  1351.5 21.2 %copy-start.6 = (f32[1,128,512]{2,1,0:T(8,128)S(1)}, f32[1,128,512]{2,1,0:T(8,128)}, u32[]{:S(2)}) copy-start(f32[1,128,512]{2,1,0:T(8,128)} %copy-done.1) | copy-start | bytes 786436
  1355.4 17.1 %all-to-all-start.11 = ((bf16[128,100,1]{1,2,0:T(2,128)(2,1)}), bf16[128,100,1]{1,2,0:T(2,128)(2,1)S(1)}, u32[]{:S(2)}, u32[]{:S(2)}) async-start(bf16[128,100,1]{1,2,0:T(2,128)(2,1)} %reshape.654), calls=%async_computation.11 | async-start | bytes 131072 | tf_op jit(solution)/shard_map/all_to_all | solution.py:121
